TPU v7x, 32 devices: a whole 2x2x4 slice. The times are simulated.
32 devices in a mesh: groups: 2 (over y), rows: 4 (over z), blocks: 2 (over x), cols: 2 (over core).
Axes of the slice: x: 2, y: 2, z: 4, core: 2. Of those that a mesh axis runs over, the one named last changes fastest.
Arguments:
- inputs: bfloat16 [4096, 1024], P(('groups', 'rows')), parts along dimension 0, may hold values from -6 to 6
- projection: bfloat16 [1024, 8192], P(None, ('groups', 'blocks', 'cols')), parts along dimension 1, may hold values from -0.1875 to 0.1875
- phases: bfloat16 [8192], P(('groups', 'blocks', 'cols')), parts along dimension 0, may hold values from -3.140625 to 3.140625
- inverse_blocks: float32 [4, 2048, 2048], P(('groups', 'blocks'), 'rows'), parts along dimension 0, as said below
- labels: int32 [4096], P(('groups', 'rows')), parts along dimension 0, may hold values from 0 to 999
- predictions: float32 [4096, 1000], P(('groups', 'rows'), 'cols'), parts along dimension 0, may hold values from -4 to 4
- coefficients: float32 [8192, 1000], P(('groups', 'blocks', 'rows'), 'cols'), parts along dimension 0, may hold values from -3 to 3
Outputs:
- new_coefficients: float32 [8192, 1000], P(('groups', 'blocks', 'rows'), 'cols'), parts along dimension 0
- new_predictions: float32 [4096, 1000], P(('groups', 'rows'), 'cols'), parts along dimension 0
There are 2 independent parts, one for each index of `groups`. A program takes and returns all parts, laid end to end along the dimension named above; each array names one. Nothing has to cross between parts.
Inputs may be any that keep to these rules, and one draw needn't show every extreme that they name: `inverse_blocks`: one dense preconditioner for each feature block.
All inputs are finite; a program needn't handle non-finite values.
Results may differ from a plain program's by a relative error of at most 0.0029.
Values may be sent and summed in bfloat16 or wider, within the bound.
No kernel may reach another device: no remote copies, remote signals or barrier semaphores. Data moves between devices by JAX's collectives and lax.ppermute only.
A program may use at most 64 MiB of HBM per device.

v0:
```python
import jax
import jax.numpy as jnp
from jax import lax
from jax.sharding import PartitionSpec as P

DAMPING = 0.5


def cosine_features(inputs, projection, phases):
    angles = (
        jnp.dot(inputs, projection, preferred_element_type=jnp.float32)
        + phases.astype(jnp.float32)[None, :]
    )
    return jnp.cos(angles).astype(jnp.bfloat16)


def shards(inputs, projection, phases, inverse_blocks, labels, predictions, coefficients):
    out_width = predictions.shape[1]
    classes = lax.axis_index("cols") * out_width + jnp.arange(out_width, dtype=jnp.int32)
    onehot = (labels[:, None] == classes[None, :]).astype(jnp.float32)
    residual = (onehot - predictions).astype(jnp.bfloat16)
    half_features = cosine_features(inputs, projection, phases)
    features_full = lax.all_gather(half_features, "cols", axis=1, tiled=True)
    local_inverse = inverse_blocks[0]
    column_slice = features_full
    own_gradient = lax.psum_scatter(
        lax.dot_general(
            column_slice, residual, (((0,), (0,)), ((), ())), preferred_element_type=jnp.float32
        ),
        "rows",
        scatter_dimension=0,
        tiled=True,
    )
    gradient = lax.all_gather(own_gradient, "rows", axis=0, tiled=True)
    solved = jnp.dot(local_inverse, gradient, precision=lax.Precision.HIGHEST)
    step_update = DAMPING * solved
    new_coefficients = coefficients + step_update
    column_slice = features_full
    contribution = jnp.dot(
        column_slice,
        lax.all_gather(step_update.astype(jnp.bfloat16), "rows", axis=0, tiled=True),
        preferred_element_type=jnp.float32,
    )
    summed = lax.psum(contribution, "blocks")
    return (new_coefficients, predictions + summed)


def solution(mesh):
    return jax.shard_map(
        shards,
        mesh=mesh,
        in_specs=(
            P(("groups", "rows"), None),
            P(None, ("groups", "blocks", "cols")),
            P(("groups", "blocks", "cols")),
            P(("groups", "blocks"), "rows", None),
            P(("groups", "rows")),
            P(("groups", "rows"), "cols"),
            P(("groups", "blocks", "rows"), "cols"),
        ),
        out_specs=(P(("groups", "blocks", "rows"), "cols"), P(("groups", "rows"), "cols")),
        check_vma=False,
    )
```

profile of v0, /device:TPU:0, one launch (start us, length us, event | category | flops | bytes accessed | tf_op | source)
XLA Modules:
  0.0 311.2 jit_solution(1773116370345842166)
XLA Ops:
  7.2 0.0 copy-start
  7.2 0.0 all-gather.4.cloned.1.call-start
  7.2 0.8 convert_element_type.15
  8.0 0.7 copy-done
  8.8 9.8 %cosine_convert_fusion = bf16[512,1024]{1,0:T(8,128)(2,1)} fusion(bf16[512,1024]{1,0:T(8,128)(2,1)} %param.7, bf16[1024,1024]{1,0:T(8,128)(2,1)S(1)} %copy-done, f32[1024]{0:T(1024)S(1)} %convert_element_type.15), kind=kOutput, calls=%fused_computation.2 | convolution fusion | flops 1074790400 | bytes 4198400 | tf_op jit(solution)/shard_map/dot_general | solution.py:11
  18.6 0.0 all-gather.4.cloned.1.call-update
  18.6 0.0 reduce-scatter.2.cloned.1.call-start
  18.7 13.4 %all-gather.4.cloned.1.call-done = bf16[512,2048]{1,0:T(8,128)(2,1)} async-done(((bf16[512,1024]{1,0:T(8,128)(2,1)}), bf16[512,2048]{1,0:T(8,128)(2,1)}) %all-gather.4.cloned.1.call-update) | async-done | bytes 2097168 | tf_op jit(solution)/shard_map/all_gather | solution.py:23
  32.1 0.0 copy-done.1
  32.1 5.0 %fusion.8 = f32[2048,500]{1,0:T(8,128)} fusion(bf16[512,2048]{1,0:T(8,128)(2,1)} %all-gather.4.cloned.1.call-done, f32[512,500]{0,1:T(8,128)S(1)} %copy-done.1, s32[512]{0:T(512)S(1)} %copy-done.2, s32[500]{0:T(512)S(1)} %iota_add_fusion), kind=kOutput, calls=%fused_computation.6 | convolution fusion | flops 1049600000 | bytes 7221200 | tf_op jit(solution)/shard_map/dot_general | solution.py:27
  37.0 0.0 reduce-scatter.2.cloned.1.call-update
  37.0 0.0 all-gather.6.cloned.1.call-start
  37.1 78.0 %reduce-scatter.2.cloned.1.call-done = f32[512,500]{1,0:T(8,128)} async-done(((f32[2048,500]{1,0:T(8,128)}), f32[512,500]{1,0:T(8,128)}) %reduce-scatter.2.cloned.1.call-update) | async-done | bytes 1024016 | tf_op jit(solution)/shard_map/reduce_scatter | solution.py:26
  115.1 0.0 all-gather.6.cloned.1.call-update
  115.2 0.2 all-gather.8.cloned.1.call-start
  115.4 82.7 %all-gather.6.cloned.1.call-done = f32[2048,500]{1,0:T(8,128)} async-done(((f32[512,500]{1,0:T(8,128)}), f32[2048,500]{1,0:T(8,128)}) %all-gather.6.cloned.1.call-update) | async-done | bytes 4096016 | tf_op jit(solution)/shard_map/all_gather | solution.py:34
  198.1 17.2 %fusion.11 = (bf16[512,500]{0,1:T(8,128)(2,1)}, f32[512,500]{0,1:T(8,128)}) fusion(f32[512,500]{0,1:T(8,128)} %param.13, f32[2048,500]{1,0:T(8,128)} %all-gather.6.cloned.1.call-done, f32[1,512,2048]{2,1,0:T(8,128)} %param.10), kind=kOutput, calls=%fused_computation.10 | convolution fusion | flops 6292224000 | bytes 10850304 | tf_op jit(solution)/shard_map/dot_general | solution.py:35
  215.3 0.0 all-gather.8.cloned.1.call-update
  215.3 0.0 all-reduce.2.cloned.1.call-start
  215.4 43.9 %all-gather.8.cloned.1.call-done = bf16[2048,500]{0,1:T(8,128)(2,1)} async-done(((bf16[512,500]{0,1:T(8,128)(2,1)}), bf16[2048,500]{0,1:T(8,128)(2,1)}) %all-gather.8.cloned.1.call-update) | async-done | bytes 2048016 | tf_op jit(solution)/shard_map/all_gather | solution.py:41
  259.3 4.4 %fusion.12 = f32[512,500]{0,1:T(8,128)} fusion(bf16[512,2048]{1,0:T(8,128)(2,1)} %all-gather.4.cloned.1.call-done, bf16[2048,500]{0,1:T(8,128)(2,1)} %all-gather.8.cloned.1.call-done), kind=kOutput, calls=%fused_computation.11 | convolution fusion | flops 1048576000 | bytes 5169152 | tf_op jit(solution)/shard_map/dot_general | solution.py:39
  263.7 0.0 all-reduce.2.cloned.1.call-update
  263.8 38.6 %all-reduce.2.cloned.1.call-done = f32[512,500]{0,1:T(8,128)} async-done(((f32[512,500]{0,1:T(8,128)}), f32[512,500]{0,1:T(8,128)}) %all-reduce.2.cloned.1.call-update) | async-done | bytes 1024016 | tf_op jit(solution)/shard_map/psum | solution.py:44
  302.3 2.4 add.33
  (4 shorter events, 0.0 us)
Async XLA Ops:
  7.2 1.6 copy-start
  7.2 24.9 %all-gather.4.cloned.1.call-start = ((), (), s32[]{:S(2)}) async-start(), calls=%async_computation.1 | async-start | bytes 3145728 | tf_op jit(solution)/shard_map/all_gather | solution.py:23
  8.8 23.3 %copy-start.1 = (f32[512,500]{0,1:T(8,128)S(1)}, f32[512,500]{0,1:T(8,128)}, u32[]{:S(2)}) copy-start(f32[512,500]{0,1:T(8,128)} %param.12) | copy-start | bytes 3072004
  8.8 23.3 %copy-start.2 = (s32[512]{0:T(512)S(1)}, s32[512]{0:T(512)}, u32[]{:S(2)}) copy-start(s32[512]{0:T(512)} %param.11) | copy-start | bytes 6148
  18.6 96.5 %reduce-scatter.2.cloned.1.call-start = ((), (), s32[]{:S(2)}) async-start(), calls=%async_computation.2 | async-start | bytes 5242880 | tf_op jit(solution)/shard_map/reduce_scatter | solution.py:26
  37.0 161.1 %all-gather.6.cloned.1.call-start = ((), (), s32[]{:S(2)}) async-start(), calls=%async_computation.3 | async-start | bytes 5242880 | tf_op jit(solution)/shard_map/all_gather | solution.py:34
  115.2 144.1 %all-gather.8.cloned.1.call-start = ((), (), s32[]{:S(2)}) async-start(), calls=%async_computation.4 | async-start | bytes 2580480 | tf_op jit(solution)/shard_map/all_gather | solution.py:41
  215.3 87.0 %all-reduce.2.cloned.1.call-start = ((), (), s32[]{:S(2)}) async-start(), calls=%async_computation.5 | async-start | bytes 2064384 | tf_op jit(solution)/shard_map/psum | solution.py:44
Sparse Core Ops, SparseCore 0:
  18.7 13.2 all-gather.3
  37.2 77.9 reduce-scatter.1
  116.8 81.2 all-gather.5
  215.4 43.8 all-gather.7
  263.9 38.3 all-reduce.1
where the time goes:
time: 311 us
  waiting for transfers between devices  257 us (83%)
  matrix products  36.4 us (12%)
  between operations  13.8 us (4%)
  other arithmetic  3.21 us (1%)
    all_gather x1, waiting for transfers between devices, shards(): gradient = lax.all_gather(own_gradient, 'rows', axis=0, tiled=True)  82.7 us
    reduce_scatter x1, waiting for transfers between devices, shards(): lax.psum_scatter(lax.dot_general(column_slice, residual, (((0,), (0,)), (...  78 us
    all_gather x1, waiting for transfers between devices, shards(): lax.all_gather(step_update.astype(jnp.bfloat16), 'rows', axis=0, tiled=True)  43.9 us
    psum x1, waiting for transfers between devices, shards(): summed = lax.psum(contribution, 'blocks')  38.6 us
    dot_general x1, matrix products, shards(): solved = jnp.dot(local_inverse, gradient, precision=lax.Precision.HIGHEST)  17.2 us
    all_gather x1, waiting for transfers between devices, shards(): features_full = lax.all_gather(half_features, 'cols', axis=1, tiled=True)  13.4 us
    dot_general x1, matrix products, cosine_features(): jnp.dot(inputs, projection, preferred_element_type=jnp.float32)  9.81 us
  transfers between devices with their start and end apart: 5, of which 5 were waited for; matrix products, arithmetic and copies ran while one was open for 0% of the time, Pallas kernels for 0%

commit v1 on v0

--- a/solution.py
+++ b/solution.py
@@ -31,7 +31,12 @@
         scatter_dimension=0,
         tiled=True,
     )
-    gradient = lax.all_gather(own_gradient, "rows", axis=0, tiled=True)
+    ring = [own_gradient]
+    for hop in range(3):
+        ring.append(lax.ppermute(ring[-1], "rows", [(dev, (dev + 1) % 4) for dev in range(4)]))
+    gradient = jnp.roll(
+        jnp.concatenate(ring[::-1], axis=0), (lax.axis_index("rows") + 1) * ring[0].shape[0], axis=0
+    )
     solved = jnp.dot(local_inverse, gradient, precision=lax.Precision.HIGHEST)
     step_update = DAMPING * solved
     new_coefficients = coefficients + step_update

time: 311 us -> 302 us (0.971)
  matrix products: 36.4 us -> 27 us
  waiting for transfers between devices: 257 us -> 248 us
  local copies, waits for them, and re-layouts: 0.74 us -> 7.84 us
    all_gather x1 -> x0, waiting for transfers between devices: 82.7 us -> none  [shards(): gradient = lax.all_gather(own_gradient, 'rows', axis=0, tiled=True)]
    ppermute x0 -> x3, waiting for transfers between devices: none -> 75.4 us  [shards(): lax.ppermute(ring[-1], 'rows', [(dev, (dev + 1) % 4) for dev in range(4)])]
    dot_general x1, matrix products: 17.2 us -> 7.93 us  [shards(): solved = jnp.dot(local_inverse, gradient, precision=lax.Precision.HIGHEST)]
    unnamed x6 -> x23, local copies, waits for them, and re-layouts: 0.74 us -> 7.75 us
  transfers between devices with their start and end apart: 5 -> 7, of which waited for: 5 -> 7; matrix products, arithmetic and copies ran while one was open for 0% -> 0% of each run, Pallas kernels for 0% -> 0%
where the time goes in v1:
time: 302 us
  waiting for transfers between devices  248 us (82%)
  matrix products  27 us (9%)
  between operations  13.9 us (5%)
  local copies, waits for them, and re-layouts  7.84 us (3%)
  other arithmetic  3.21 us (1%)
    reduce_scatter x1, waiting for transfers between devices, shards(): lax.psum_scatter(lax.dot_general(column_slice, residual, (((0,), (0,)), (...  77 us
    ppermute x3, waiting for transfers between devices, shards(): lax.ppermute(ring[-1], 'rows', [(dev, (dev + 1) % 4) for dev in range(4)])  75.4 us
    all_gather x1, waiting for transfers between devices, shards(): lax.all_gather(step_update.astype(jnp.bfloat16), 'rows', axis=0, tiled=True)  43.5 us
    psum x1, waiting for transfers between devices, shards(): summed = lax.psum(contribution, 'blocks')  38.6 us
    all_gather x1, waiting for transfers between devices, shards(): features_full = lax.all_gather(half_features, 'cols', axis=1, tiled=True)  13.4 us
    dot_general x1, matrix products, cosine_features(): jnp.dot(inputs, projection, preferred_element_type=jnp.float32)  9.82 us
    dot_general x1, matrix products, shards(): solved = jnp.dot(local_inverse, gradient, precision=lax.Precision.HIGHEST)  7.93 us
    unnamed x23, local copies, waits for them, and re-layouts  7.75 us
  transfers between devices with their start and end apart: 7, of which 7 were waited for; matrix products, arithmetic and copies ran while one was open for 0% of the time, Pallas kernels for 0%

profile of v1, /device:TPU:0, one launch (start us, length us, event | category | flops | bytes accessed | tf_op | source)
XLA Modules:
  0.0 301.5 jit_solution(2785223272854950324)
XLA Ops:
  7.2 0.8 convert_element_type.15
  8.0 0.7 copy-done
  8.8 9.8 %cosine_convert_fusion = bf16[512,1024]{1,0:T(8,128)(2,1)} fusion(bf16[512,1024]{1,0:T(8,128)(2,1)} %param.7, bf16[1024,1024]{1,0:T(8,128)(2,1)S(1)} %copy-done, f32[1024]{0:T(1024)S(1)} %convert_element_type.15), kind=kOutput, calls=%fused_computation.3 | convolution fusion | flops 1074790400 | bytes 4198400 | tf_op jit(solution)/shard_map/dot_general | solution.py:11
  18.7 13.4 %all-gather.3.cloned.1.call-done = bf16[512,2048]{1,0:T(8,128)(2,1)} async-done(((bf16[512,1024]{1,0:T(8,128)(2,1)}), bf16[512,2048]{1,0:T(8,128)(2,1)}) %all-gather.3.cloned.1.call-update) | async-done | bytes 2097168 | tf_op jit(solution)/shard_map/all_gather | solution.py:23
  32.1 4.8 %fusion.13 = f32[2048,500]{0,1:T(8,128)} fusion(bf16[512,2048]{1,0:T(8,128)(2,1)} %all-gather.3.cloned.1.call-done, f32[512,500]{0,1:T(8,128)S(1)} %copy-done.2, s32[512]{0:T(512)S(1)} %copy-done.7, s32[500]{0:T(512)S(1)} %iota_add_fusion), kind=kOutput, calls=%fused_computation.7 | convolution fusion | flops 1049600000 | bytes 7221200 | tf_op jit(solution)/shard_map/dot_general | solution.py:27
  36.9 77.0 %reduce-scatter.2.cloned.1.call-done = f32[512,500]{0,1:T(8,128)} async-done(((f32[2048,500]{0,1:T(8,128)}), f32[512,500]{0,1:T(8,128)}) %reduce-scatter.2.cloned.1.call-update) | async-done | bytes 1024016 | tf_op jit(solution)/shard_map/reduce_scatter | solution.py:26
  114.0 1.4 collective-permute-start
  115.4 25.1 %collective-permute-done = f32[512,500]{0,1:T(8,128)S(1)} collective-permute-done((f32[512,500]{0,1:T(8,128)}, f32[512,500]{0,1:T(8,128)S(1)}, u32[]{:S(2)}, u32[]{:S(2)}) %collective-permute-start) | collective-permute-done | bytes 1024032 | tf_op jit(solution)/shard_map/ppermute | solution.py:36
  140.5 1.0 copy-done.4
  141.4 25.5 %collective-permute-done.1 = f32[512,500]{0,1:T(8,128)} collective-permute-done((f32[512,500]{0,1:T(8,128)S(1)}, f32[512,500]{0,1:T(8,128)}, u32[]{:S(2)}, u32[]{:S(2)}) %collective-permute-start.1) | collective-permute-done | bytes 1024032 | tf_op jit(solution)/shard_map/ppermute | solution.py:36
  167.0 24.8 %collective-permute-done.2 = f32[512,500]{0,1:T(8,128)} collective-permute-done((f32[512,500]{0,1:T(8,128)}, f32[512,500]{0,1:T(8,128)}, u32[]{:S(2)}, u32[]{:S(2)}) %collective-permute-start.2) | collective-permute-done | bytes 1024032 | tf_op jit(solution)/shard_map/ppermute | solution.py:36
  191.8 1.3 constant_dynamic-update-slice_fusion.7
  193.1 1.3 constant_dynamic-update-slice_fusion.6
  194.4 0.1 constant_dynamic-update-slice_fusion.5
  194.5 0.1 constant_dynamic-update-slice_fusion.4
  194.6 1.5 constant_dynamic-update-slice_fusion.3
  196.1 1.7 constant_dynamic-update-slice_fusion.2
  197.8 0.1 constant_dynamic-update-slice_fusion.1
  197.9 0.1 constant_dynamic-update-slice_fusion
  198.0 7.9 %fusion.17 = (bf16[512,500]{0,1:T(8,128)(2,1)}, f32[512,500]{0,1:T(8,128)}) fusion(f32[512,500]{0,1:T(8,128)S(1)} %copy-done.6, f32[1,512,2048]{2,1,0:T(8,128)S(1)} %copy-done.1, f32[4096,500]{0,1:T(8,128)S(1)} %constant_dynamic-update-slice_fusion, s32[]{:T(128)S(6)} %select_n.14), kind=kOutput, calls=%fused_computation.20 | convolution fusion | flops 6292224000 | bytes 10891268 | tf_op jit(solution)/shard_map/dot_general | solution.py:40
  206.0 43.5 %all-gather.5.cloned.1.call-done = bf16[2048,500]{0,1:T(8,128)(2,1)} async-done(((bf16[512,500]{0,1:T(8,128)(2,1)}), bf16[2048,500]{0,1:T(8,128)(2,1)}) %all-gather.5.cloned.1.call-update) | async-done | bytes 2048016 | tf_op jit(solution)/shard_map/all_gather | solution.py:46
  249.6 4.4 %fusion.18 = f32[512,500]{0,1:T(8,128)} fusion(bf16[512,2048]{1,0:T(8,128)(2,1)} %all-gather.3.cloned.1.call-done, bf16[2048,500]{0,1:T(8,128)(2,1)} %all-gather.5.cloned.1.call-done), kind=kOutput, calls=%fused_computation.21 | convolution fusion | flops 1048576000 | bytes 5169152 | tf_op jit(solution)/shard_map/dot_general | solution.py:44
  254.0 38.6 %all-reduce.2.cloned.1.call-done = f32[512,500]{0,1:T(8,128)} async-done(((f32[512,500]{0,1:T(8,128)}), f32[512,500]{0,1:T(8,128)}) %all-reduce.2.cloned.1.call-update) | async-done | bytes 1024016 | tf_op jit(solution)/shard_map/psum | solution.py:49
  292.6 2.4 add.49
  (25 shorter events, 0.3 us)
Async XLA Ops:
  7.2 1.6 copy-start
  7.2 24.9 %all-gather.3.cloned.1.call-start = ((), (), s32[]{:S(2)}) async-start(), calls=%async_computation.1 | async-start | bytes 3145728 | tf_op jit(solution)/shard_map/all_gather | solution.py:23
  8.8 23.3 %copy-start.2 = (f32[512,500]{0,1:T(8,128)S(1)}, f32[512,500]{0,1:T(8,128)}, u32[]{:S(2)}) copy-start(f32[512,500]{0,1:T(8,128)} %param.12) | copy-start | bytes 3072004
  8.8 23.3 %copy-start.7 = (s32[512]{0:T(512)S(1)}, s32[512]{0:T(512)}, u32[]{:S(2)}) copy-start(s32[512]{0:T(512)} %param.11) | copy-start | bytes 6148
  18.6 95.3 %reduce-scatter.2.cloned.1.call-start = ((), (), s32[]{:S(2)}) async-start(), calls=%async_computation.2 | async-start | bytes 5160960 | tf_op jit(solution)/shard_map/reduce_scatter | solution.py:26
  36.9 212.7 %all-gather.5.cloned.1.call-start = ((), (), s32[]{:S(2)}) async-start(), calls=%async_computation.3 | async-start | bytes 2580480 | tf_op jit(solution)/shard_map/all_gather | solution.py:46
  114.0 26.5 %collective-permute-start = (f32[512,500]{0,1:T(8,128)}, f32[512,500]{0,1:T(8,128)S(1)}, u32[]{:S(2)}, u32[]{:S(2)}) collective-permute-start(f32[512,500]{0,1:T(8,128)} %reduce-scatter.2.cloned.1.call-done), channel_id=1, source_target_pairs={{0,4},{4,8},{8,12},{12,0},{1,5},{5,9},{9,13},{13,1},{2,6},{6,10},{... | collective-permute-start | bytes 3072008 | tf_op jit(solution)/shard_map/ppermute | solution.py:36
  140.5 1.0 copy-start.4
  141.4 25.5 %collective-permute-start.1 = (f32[512,500]{0,1:T(8,128)S(1)}, f32[512,500]{0,1:T(8,128)}, u32[]{:S(2)}, u32[]{:S(2)}) collective-permute-start(f32[512,500]{0,1:T(8,128)S(1)} %collective-permute-done), channel_id=1, source_target_pairs={{0,4},{4,8},{8,12},{12,0},{1,5},{5,9},{9,13},{13,1},{2,6},{6,10},{... | collective-permute-start | bytes 3072008 | tf_op jit(solution)/shard_map/ppermute | solution.py:36
  167.0 24.8 %collective-permute-start.2 = (f32[512,500]{0,1:T(8,128)}, f32[512,500]{0,1:T(8,128)}, u32[]{:S(2)}, u32[]{:S(2)}) collective-permute-start(f32[512,500]{0,1:T(8,128)} %collective-permute-done.1), channel_id=1, source_target_pairs={{0,4},{4,8},{8,12},{12,0},{1,5},{5,9},{9,13},{13,1},{2,6},{6,10},{... | collective-permute-start | bytes 3072008 | tf_op jit(solution)/shard_map/ppermute | solution.py:36
  167.0 27.4 %copy-start.5 = (f32[512,500]{0,1:T(8,128)S(1)}, f32[512,500]{0,1:T(8,128)}, u32[]{:S(2)}) copy-start(f32[512,500]{0,1:T(8,128)} %copy-done.4) | copy-start | bytes 3072004
  167.0 27.5 %copy-start.3 = (f32[512,500]{0,1:T(8,128)S(1)}, f32[512,500]{0,1:T(8,128)}, u32[]{:S(2)}) copy-start(f32[512,500]{0,1:T(8,128)} %reduce-scatter.2.cloned.1.call-done) | copy-start | bytes 3072004
  194.6 3.4 %copy-start.1 = (f32[1,512,2048]{2,1,0:T(8,128)S(1)}, f32[1,512,2048]{2,1,0:T(8,128)}, u32[]{:S(2)}) copy-start(f32[1,512,2048]{2,1,0:T(8,128)} %param.10) | copy-start | bytes 12582916
  194.6 3.4 %copy-start.6 = (f32[512,500]{0,1:T(8,128)S(1)}, f32[512,500]{0,1:T(8,128)}, u32[]{:S(2)}) copy-start(f32[512,500]{0,1:T(8,128)} %param.13) | copy-start | bytes 3072004
  206.0 86.6 %all-reduce.2.cloned.1.call-start = ((), (), s32[]{:S(2)}) async-start(), calls=%async_computation.4 | async-start | bytes 2064384 | tf_op jit(solution)/shard_map/psum | solution.py:49
Sparse Core Ops, SparseCore 0:
  18.8 13.2 all-gather.2
  37.0 76.8 reduce-scatter.1
  206.1 43.4 all-gather.4
  254.2 38.3 all-reduce.1
